TPU v7x, 32 devices: a whole 2x2x4 slice. The times are simulated.
32 devices in a mesh: ex: 8 (over z, y), tp: 4 (over x, core).
Axes of the slice: x: 2, y: 2, z: 4, core: 2. Of those that a mesh axis runs over, the one named last changes fastest.
Arguments:
- residual_in: bfloat16 [1536, 2880], P('ex', 'tp'), may hold values from -40 to 40
- queries: bfloat16 [1536, 2048], P('ex', 'tp'), may hold values from -4 to 4
- keys_values: bfloat16 [1536, 4, 128], P('ex', 'tp'), may hold values from -4 to 4
- sink_logits: float32 [32], P('tp'), may hold values from 1 to 6
- out_proj: bfloat16 [2048, 2880], P('tp'), may hold values from -0.75 to 0.75
- norm_gain: float32 [2880], replicated, may hold values from 0.25 to 1.75
- routes: int32 [1536, 4], P('ex'), may hold values from 0 to 7, all different within a row; in each aligned block of 192 rows (0 to 191, 192 to 383, ...) at most 160 rows name the same one
- route_scores: int32 [1536, 4], P('ex'), may hold values from 1 to 8
- tenants: int32 [1536], P('ex'), may hold values from 0 to 7
- gate_up: bfloat16 [8, 2880, 2, 1536], P('ex', None, None, 'tp'), may hold values from -0.109375 to 0.109375
- adapter_in: bfloat16 [8, 2880, 128], P('ex'), may hold values from -0.109375 to 0.109375
- adapter_out: bfloat16 [8, 128, 2, 1536], P('ex', None, None, 'tp'), may hold values from -1.5 to 1.5
- down_proj: bfloat16 [8, 1536, 2880], P('ex', 'tp'), may hold values from -0.15625 to 0.15625
Outputs:
- residual_out: bfloat16 [1536, 2880], P('ex', 'tp')
- expert_mix: bfloat16 [1536, 2880], P('ex', 'tp')
Inputs may be any that keep to these rules, and one draw needn't show every extreme that they name: `routes`: among the 192 rows of one device (aligned blocks), no expert is named by more than 160 rows, and in every draw some expert is named by exactly 160 rows of some block.
All inputs are finite; a program needn't handle non-finite values.
Results may differ from a plain program's by a relative error of at most 0.023.
Values may be sent and summed in bfloat16 or wider, within the bound.
A program may use at most 128 MiB of HBM per device.

v0:
```python
import jax
import jax.numpy as jnp
from jax import lax
from jax.sharding import PartitionSpec as P

WINDOW = 128
TOP = 4
RANK = 16


def from_behind(value, axis, steps):
    count = lax.axis_size(axis)
    initial, last = (max(0, -steps), min(count, count - steps))
    return lax.ppermute(value, axis, [(source, source + steps) for source in range(initial, last)])


def shards(
    residual_in,
    queries,
    keys_values,
    sink_logits,
    out_proj,
    norm_gain,
    routes,
    route_scores,
    tenants,
    gate_up,
    adapter_in,
    adapter_out,
    down_proj,
):
    tok_rows = residual_in.shape[0]
    columns = residual_in.shape[1]
    width = out_proj.shape[1]
    heads_here = sink_logits.shape[0]
    kv_here = keys_values.shape[1]
    group_size = heads_here // kv_here
    head_size = keys_values.shape[2] // 2
    rim_rows = WINDOW - 1
    table = token_table(routes, route_scores, tenants, gate_up.shape[0] * lax.axis_size("ex"))
    before = from_behind(keys_values[tok_rows - rim_rows :], "ex", 1)
    extended = jnp.concatenate([before, keys_values], axis=0)
    keys_only = extended[:, :, :head_size]
    values_only = extended[:, :, head_size:]
    query_rows = queries.reshape(tok_rows, kv_here, group_size, head_size)
    scores = jnp.einsum(
        "tcgd,jcd->cgtj", query_rows, keys_only, preferred_element_type=jnp.float32
    ) * head_size ** (-0.5)
    start = lax.axis_index("ex") * tok_rows
    query_pos = start + jnp.arange(tok_rows, dtype=jnp.int32)
    key_pos = start - rim_rows + jnp.arange(tok_rows + rim_rows, dtype=jnp.int32)
    distance = query_pos[:, None] - key_pos[None, :]
    allowed = (distance >= 0) & (distance < WINDOW) & (key_pos[None, :] >= 0)
    numerators = jnp.where(allowed, jnp.exp(scores), 0.0)
    totals = jnp.exp(sink_logits.reshape(kv_here, group_size))[:, :, None] + jnp.sum(
        numerators, axis=-1
    )
    weights = (numerators / totals[..., None]).astype(jnp.bfloat16)
    attended = jnp.einsum(
        "cgtj,jcd->tcgd", weights, values_only, preferred_element_type=jnp.float32
    )
    attended = attended.astype(jnp.bfloat16).reshape(tok_rows, heads_here * head_size)
    head_terms = jnp.dot(attended, out_proj, preferred_element_type=jnp.float32)
    head_share = lax.psum_scatter(
        head_terms.astype(jnp.bfloat16), "tp", scatter_dimension=1, tiled=True
    ).astype(jnp.float32)
    residual_out = (residual_in.astype(jnp.float32) + head_share).astype(jnp.bfloat16)
    sources = lax.axis_size("ex")
    experts_all = gate_up.shape[0] * sources
    capacity = 5 * tok_rows * TOP // (3 * experts_all)
    if gate_up.shape[0] == 1 and 2 * capacity >= tok_rows:
        mixed = dense_experts(
            residual_out, table, norm_gain, gate_up, adapter_in, adapter_out, down_proj
        )
        return (residual_out, mixed)
    return (
        residual_out,
        routed_experts(
            residual_out,
            norm_gain,
            routes,
            route_scores,
            tenants,
            gate_up,
            adapter_in,
            adapter_out,
            down_proj,
            columns,
        ),
    )


def token_table(routes, route_scores, tenants, experts_all):
    score_float = route_scores.astype(jnp.float32)
    share = score_float / jnp.sum(score_float, axis=1, keepdims=True)
    hit = routes[:, :, None] == jnp.arange(experts_all, dtype=jnp.int32)[None, None, :]
    by_expert = jnp.sum(jnp.where(hit, share[:, :, None], 0.0), axis=1)
    return jnp.concatenate([by_expert, tenants.astype(jnp.float32)[:, None]], axis=1)


def dense_experts(residual_out, table, norm_gain, gate_up, adapter_in, adapter_out, down_proj):
    tok_rows, columns = residual_out.shape
    sources = lax.axis_size("ex")
    quarters = lax.axis_size("tp")
    width = columns * quarters
    rows_all = sources * tok_rows
    hidden_here = gate_up.shape[3]
    rank_cols = adapter_in.shape[2]
    tokens = gather_tokens(residual_out)
    whole_rows = tokens.astype(jnp.float32)
    inverse = lax.rsqrt(jnp.mean(whole_rows * whole_rows, axis=-1, keepdims=True) + 1e-05)
    normed = (whole_rows * inverse * norm_gain).astype(jnp.bfloat16)
    everyone = lax.all_gather(table, "ex", axis=0, tiled=True)
    expert = lax.axis_index("ex")
    here = jnp.arange(everyone.shape[1], dtype=jnp.int32)[None, :] == expert
    weight = jnp.sum(jnp.where(here, everyone, 0.0), axis=1, keepdims=True)
    tenant = everyone[:, -1:].astype(jnp.int32)
    mapped = jnp.dot(
        normed, gate_up[0].reshape(width, 2 * hidden_here), preferred_element_type=jnp.float32
    )
    low_rank = jnp.dot(normed, adapter_in[0], preferred_element_type=jnp.float32)
    keep = (jnp.arange(rank_cols, dtype=jnp.int32) // RANK)[None, :] == tenant
    low_rank = jnp.where(keep, low_rank, 0.0).astype(jnp.bfloat16)
    mapped = mapped + jnp.dot(
        low_rank,
        adapter_out[0].reshape(rank_cols, 2 * hidden_here),
        preferred_element_type=jnp.float32,
    )
    gate_part = mapped[:, :hidden_here]
    up_part = mapped[:, hidden_here:]
    activated = (gate_part * jax.nn.sigmoid(1.702 * gate_part) * (up_part + 1.0) * weight).astype(
        jnp.bfloat16
    )
    terms = jnp.dot(activated, down_proj[0], preferred_element_type=jnp.float32).astype(
        jnp.bfloat16
    )
    return scatter_terms(terms)


def gather_tokens(residual_out):
    tok_rows, columns = residual_out.shape
    sources, quarters = (lax.axis_size("ex"), lax.axis_size("tp"))
    blocks = lax.all_gather(residual_out, ("ex", "tp"), axis=0, tiled=False)
    blocks = blocks.reshape(sources, quarters, tok_rows, columns).transpose(0, 2, 1, 3)
    return blocks.reshape(sources * tok_rows, quarters * columns)


def scatter_terms(terms):
    mine = lax.psum_scatter(terms, "tp", scatter_dimension=1, tiled=True)
    return lax.psum_scatter(mine, "ex", scatter_dimension=0, tiled=True)


def routed_experts(
    residual_out,
    norm_gain,
    routes,
    route_scores,
    tenants,
    gate_up,
    adapter_in,
    adapter_out,
    down_proj,
    columns,
):
    tok_rows = residual_out.shape[0]
    width = gate_up.shape[1]
    whole_rows = lax.all_gather(residual_out, "tp", axis=1, tiled=True).astype(jnp.float32)
    inverse = lax.rsqrt(jnp.mean(whole_rows * whole_rows, axis=-1, keepdims=True) + 1e-05)
    normed = (whole_rows * inverse * norm_gain).astype(jnp.bfloat16)
    sources = lax.axis_size("ex")
    local_count = gate_up.shape[0]
    experts_all = local_count * sources
    capacity = 5 * tok_rows * TOP // (3 * experts_all)
    pair_count = tok_rows * TOP
    route_flat = routes.reshape(pair_count)
    one_hot = (route_flat[:, None] == jnp.arange(experts_all, dtype=jnp.int32)[None, :]).astype(
        jnp.int32
    )
    earlier = jnp.cumsum(one_hot, axis=0) - one_hot
    slot = jnp.sum(earlier * one_hot, axis=1)
    target = route_flat * capacity + slot
    pair_of = (
        jnp.full((experts_all * capacity,), pair_count, jnp.int32)
        .at[target]
        .set(jnp.arange(pair_count, dtype=jnp.int32))
    )
    token_of = pair_of // TOP
    send_width = normed.shape[1]
    normed_pad = jnp.concatenate([normed, jnp.zeros((1, send_width), jnp.bfloat16)], axis=0)
    tenant_pad = jnp.concatenate([tenants, jnp.zeros((1,), jnp.int32)])
    sent_rows = normed_pad[token_of].reshape(experts_all, capacity, send_width)
    sent_tenants = tenant_pad[token_of].reshape(experts_all, capacity)
    received, got_tenants = (
        lax.all_to_all(sent_rows, "ex", split_axis=0, concat_axis=0, tiled=True),
        lax.all_to_all(sent_tenants, "ex", split_axis=0, concat_axis=0, tiled=True),
    )
    hidden_here = gate_up.shape[3]
    rank_cols = adapter_in.shape[2]
    arrived = received.reshape(sources, local_count, capacity, width)
    arrived_tenants = got_tenants.reshape(sources, local_count, capacity)
    slot_rows = arrived[:, 0].reshape(sources * capacity, width)
    slot_tenant = arrived_tenants[:, 0].reshape(sources * capacity)
    mapped = jnp.dot(
        slot_rows, gate_up[0].reshape(width, 2 * hidden_here), preferred_element_type=jnp.float32
    )
    low_rank = jnp.dot(slot_rows, adapter_in[0], preferred_element_type=jnp.float32)
    keep = (jnp.arange(rank_cols, dtype=jnp.int32) // RANK)[None, :] == slot_tenant[:, None]
    low_rank = jnp.where(keep, low_rank, 0.0).astype(jnp.bfloat16)
    mapped = mapped + jnp.dot(
        low_rank,
        adapter_out[0].reshape(rank_cols, 2 * hidden_here),
        preferred_element_type=jnp.float32,
    )
    gate_part = mapped[:, :hidden_here]
    up_part = mapped[:, hidden_here:]
    activated = (gate_part * jax.nn.sigmoid(1.702 * gate_part) * (up_part + 1.0)).astype(
        jnp.bfloat16
    )
    quarter = jnp.dot(activated, down_proj[0], preferred_element_type=jnp.float32).astype(
        jnp.bfloat16
    )
    outputs = quarter.reshape(sources, 1, capacity, width)
    quarters = outputs.reshape(sources * local_count, capacity, width)
    score_float = route_scores.astype(jnp.float32)
    route_weight = (score_float / jnp.sum(score_float, axis=1, keepdims=True)).reshape(pair_count)
    shares = lax.psum_scatter(
        quarters.astype(jnp.float32).astype(jnp.bfloat16), "tp", scatter_dimension=2, tiled=True
    ).astype(jnp.float32)
    returned = lax.all_to_all(
        shares.astype(jnp.bfloat16), "ex", split_axis=0, concat_axis=0, tiled=True
    ).astype(shares.dtype)
    picked = returned.reshape(experts_all * capacity, columns)[target]
    expert_mix = jnp.sum((picked * route_weight[:, None]).reshape(tok_rows, TOP, columns), axis=1)
    return expert_mix.astype(jnp.bfloat16)


def solution(mesh):
    in_specs = (
        P("ex", "tp"),
        P("ex", "tp"),
        P("ex", "tp", None),
        P("tp"),
        P("tp", None),
        P(),
        P("ex", None),
        P("ex", None),
        P("ex"),
        P("ex", None, None, "tp"),
        P("ex", None, None),
        P("ex", None, None, "tp"),
        P("ex", "tp", None),
    )
    out_specs = (P("ex", "tp"), P("ex", "tp"))
    return jax.shard_map(shards, mesh=mesh, in_specs=in_specs, out_specs=out_specs, check_vma=False)
```

profile of v0, /device:TPU:0, one launch (start us, length us, event | category | flops | bytes accessed | tf_op | source)
XLA Modules:
  0.0 385.4 jit_solution(12304677267419445353)
XLA Ops:
  7.2 1.0 copy.43
  8.3 0.1 slice.24
  8.4 4.9 %collective-permute-start = (bf16[127,1,128]{0,2,1:T(8,128)(2,1)S(1)}, bf16[127,1,128]{0,2,1:T(8,128)(2,1)S(1)}, u32[]{:S(2)}, u32[]{:S(2)}) collective-permute-start(bf16[127,1,128]{0,2,1:T(8,128)(2,1)S(1)} %slice.24), channel_id=1, source_target_pairs={{0,4},{4,8},{8,12},{12,16},{16,20},{20,24},{24,28},{1,5},{5,9},{9,... | collective-permute-start | bytes 97544 | tf_op jit(solution)/shard_map/ppermute | solution.py:14
  13.3 0.1 fusion.21
  13.5 1.1 copy.45
  14.5 0.7 exp.19
  15.2 0.9 fusion.8
  16.1 0.1 broadcast_add_fusion
  16.2 0.8 convolution_convert_fusion.2
  17.0 2.1 convolution_convert_fusion.1
  19.2 2.5 copy.49
  21.7 0.0 all-gather.4.cloned.1.call-start
  21.8 29.2 %reduce-scatter.10.cloned.1.call-done = bf16[720,192]{1,0:T(8,128)(2,1)} async-done(((bf16[2880,192]{1,0:T(8,128)(2,1)}), bf16[720,192]{1,0:T(8,128)(2,1)}) %reduce-scatter.10.cloned.1.call-update) | async-done | bytes 276496
  51.0 1.1 copy.50
  52.1 0.8 add_convert_fusion
  52.9 0.0 reduce-scatter.8.cloned.1.call-start
  53.0 0.1 mul.66
  53.1 5.2 %copy.53 = bf16[360,8,2,384]{3,1,2,0:T(8,128)(2,1)} copy(bf16[360,8,2,384]{3,2,1,0:T(2,128)(2,1)} %bitcast.65) | data formatting | bytes 8847360
  58.4 31.1 %all-gather.1 = f32[8,192,9]{1,2,0:T(8,128)S(1)} all-gather(f32[1,192,9]{1,2,0:T(8,128)S(1)} %maximum_bitcast_fusion), channel_id=1, replica_groups=mesh['ex'=8,'tp'=4] {'ex'}, dimensions={0}, use_global_device_ids=true | all-gather | bytes 62208 | tf_op jit(solution)/shard_map/all_gather | solution.py:113
  89.5 0.1 reshape.136
  89.7 0.1 select_reduce_fusion
  89.8 46.3 %all-gather.4.cloned.1.call-done = bf16[6144,720]{1,0:T(8,128)(2,1)} async-done(((bf16[192,720]{1,0:T(8,128)(2,1)}), bf16[6144,720]{1,0:T(8,128)(2,1)}) %all-gather.4.cloned.1.call-update) | async-done | bytes 8847376 | tf_op jit(solution)/shard_map/all_gather | solution.py:143
  136.1 12.6 %convert.1 = f32[8,4,192,720]{3,2,1,0:T(8,128)} convert(bf16[8,4,192,720]{3,2,1,0:T(8,128)(2,1)} %bitcast.62) | non-fusion elementwise | flops 4423680 | bytes 26542080 | tf_op jit(solution)/shard_map/convert_element_type | solution.py:110
  148.7 5.8 %multiply_reduce_fusion = f32[8,192]{1,0:T(8,128)S(1)} fusion(bf16[8,4,192,720]{3,2,1,0:T(8,128)(2,1)} %bitcast.63), kind=kLoop, calls=%fused_computation.3 | loop fusion | flops 13269504 | bytes 8853504 | tf_op jit(solution)/shard_map/reduce_sum | solution.py:111
  154.5 23.8 %fusion.2 = bf16[8,192,4,720]{3,2,1,0:T(4,128)(2,1)} fusion(f32[8,4,192,720]{3,2,1,0:T(8,128)} %convert.1, f32[4,720]{1,0:T(4,128)S(1)} %mul.66, f32[8,192]{1,0:T(8,128)S(1)} %add_rsqrt_fusion), kind=kLoop, calls=%fused_computation.5 | loop fusion | flops 13271040 | bytes 26559744 | tf_op jit(solution)/shard_map/convert_element_type | solution.py:112
  178.3 17.7 %convert_element_type.74 = bf16[1536,2880]{1,0:T(8,128)(2,1)} reshape(bf16[8,192,4,720]{3,2,1,0:T(4,128)(2,1)} %fusion.2) | data formatting | bytes 17694720 | tf_op jit(solution)/shard_map/convert_element_type | solution.py:112
  196.1 12.8 %fusion.37 = f32[1536,768]{1,0:T(8,128)} fusion(bf16[1536,2880]{1,0:T(8,128)(2,1)} %convert_element_type.74, bf16[2880,768]{1,0:T(8,128)(2,1)} %bitcast.66), kind=kOutput, calls=%fused_computation.66 | convolution fusion | flops 6794772480 | bytes 17989632 | tf_op jit(solution)/shard_map/dot_general | solution.py:118
  208.9 11.2 %convolution_add_fusion = f32[1536,768]{1,0:T(8,128)} fusion(f32[1536,768]{1,0:T(8,128)} %fusion.37, bf16[128,768]{1,0:T(8,128)(2,1)S(1)} %bitcast.67, bf16[1536,2880]{1,0:T(8,128)(2,1)} %convert_element_type.74, bf16[1,2880,128]{2,1,0:T(8,128)(2,1)S(1)} %copy-done.2, s32[128]{0:T(128)S(1)} %and_select_fusion, s32[1536]{0:T(1024)S(1)} %fusion.29), kind=kOutput, calls=%fused_computation.6 | convolution fusion | flops 1436221440 | bytes 19225088 | tf_op jit(solution)/shard_map/dot_general | solution.py:124
  220.1 11.5 %convolution_convert_fusion = bf16[1536,2880]{0,1:T(8,128)(2,1)} fusion(bf16[1,384,2880]{1,2,0:T(8,128)(2,1)} %param.25, f32[1536,768]{1,0:T(8,128)} %convolution_add_fusion, f32[1536]{0:T(1024)S(1)} %select_reduce_fusion), kind=kOutput, calls=%fused_computation.4 | convolution fusion | flops 3407118336 | bytes 15783936 | tf_op jit(solution)/shard_map/dot_general | solution.py:134
  231.6 72.8 %reduce-scatter.8.cloned.1.call-done = bf16[1536,720]{0,1:T(8,128)(2,1)} async-done(((bf16[1536,2880]{0,1:T(8,128)(2,1)}), bf16[1536,720]{0,1:T(8,128)(2,1)}) %reduce-scatter.8.cloned.1.call-update) | async-done | bytes 2211856 | tf_op jit(solution)/shard_map/reduce_scatter | solution.py:149
  304.5 4.2 %copy.51 = bf16[1536,720]{1,0:T(8,128)(2,1)} copy(bf16[1536,720]{0,1:T(8,128)(2,1)} %reduce-scatter.8.cloned.1.call-done) | data formatting | bytes 4423680
  308.7 70.1 %reduce-scatter.12.cloned.1.call-done = bf16[192,720]{1,0:T(8,128)(2,1)} async-done(((bf16[1536,720]{1,0:T(8,128)(2,1)}), bf16[192,720]{1,0:T(8,128)(2,1)}) %reduce-scatter.12.cloned.1.call-update) | async-done | bytes 276496
  (39 shorter events, 0.4 us)
Async XLA Ops:
  7.2 9.9 %copy-start = (bf16[512,2880]{0,1:T(8,128)(2,1)S(1)}, bf16[512,2880]{0,1:T(8,128)(2,1)}, u32[]{:S(2)}) copy-start(bf16[512,2880]{0,1:T(8,128)(2,1)} %param.17) | copy-start | bytes 8847364
  7.2 43.8 %reduce-scatter.10.cloned.1.call-start = ((), (), s32[]{:S(2)}) async-start(), calls=%async_computation.5 | async-start | bytes 1843200
  8.4 6.8 %collective-permute-start = (bf16[127,1,128]{0,2,1:T(8,128)(2,1)S(1)}, bf16[127,1,128]{0,2,1:T(8,128)(2,1)S(1)}, u32[]{:S(2)}, u32[]{:S(2)}) collective-permute-start(bf16[127,1,128]{0,2,1:T(8,128)(2,1)S(1)} %slice.24), channel_id=1, source_target_pairs={{0,4},{4,8},{8,12},{12,16},{16,20},{20,24},{24,28},{1,5},{5,9},{9,... | collective-permute-start | bytes 97544 | tf_op jit(solution)/shard_map/ppermute | solution.py:14
  19.1 33.0 %copy-start.3 = (bf16[192,720]{1,0:T(8,128)(2,1)S(1)}, bf16[192,720]{1,0:T(8,128)(2,1)}, u32[]{:S(2)}) copy-start(bf16[192,720]{1,0:T(8,128)(2,1)} %param.13) | copy-start | bytes 829444
  19.2 33.8 %copy-start.6 = (f32[2880]{0:T(1024)S(1)}, f32[2880]{0:T(1024)}, u32[]{:S(2)}) copy-start(f32[2880]{0:T(1024)} %param.18) | copy-start | bytes 34564
  21.7 114.4 %all-gather.4.cloned.1.call-start = ((), (), s32[]{:S(2)}) async-start(), calls=%async_computation.4 | async-start | bytes 9732096 | tf_op jit(solution)/shard_map/all_gather | solution.py:143
  52.9 251.6 %reduce-scatter.8.cloned.1.call-start = ((), (), s32[]{:S(2)}) async-start(), calls=%async_computation.3 | async-start | bytes 11059200 | tf_op jit(solution)/shard_map/reduce_scatter | solution.py:149
  53.1 5.2 %copy-start.8 = (s32[192]{0:T(256)S(1)}, s32[192]{0:T(256)}, u32[]{:S(2)}) copy-start(s32[192]{0:T(256)} %param.21) | copy-start | bytes 2308
  53.1 5.2 %copy-start.5 = (s32[192,4]{0,1:T(4,128)S(1)}, s32[192,4]{0,1:T(4,128)}, u32[]{:S(2)}) copy-start(s32[192,4]{0,1:T(4,128)} %param.20) | copy-start | bytes 9220
  53.1 5.2 %copy-start.7 = (s32[192,4]{0,1:T(4,128)S(1)}, s32[192,4]{0,1:T(4,128)}, u32[]{:S(2)}) copy-start(s32[192,4]{0,1:T(4,128)} %param.19) | copy-start | bytes 9220
  53.1 36.5 %copy-start.4 = (bf16[1,128,2,384]{3,2,1,0:T(2,128)(2,1)S(1)}, bf16[1,128,2,384]{3,2,1,0:T(2,128)(2,1)}, u32[]{:S(2)}) copy-start(bf16[1,128,2,384]{3,2,1,0:T(2,128)(2,1)} %param.24) | copy-start | bytes 589828
  196.1 12.8 %copy-start.2 = (bf16[1,2880,128]{2,1,0:T(8,128)(2,1)S(1)}, bf16[1,2880,128]{2,1,0:T(8,128)(2,1)}, u32[]{:S(2)}) copy-start(bf16[1,2880,128]{2,1,0:T(8,128)(2,1)} %param.23) | copy-start | bytes 2211844
  231.6 147.2 %copy-start.1 = (bf16[512,2880]{0,1:T(8,128)(2,1)S(1)}, bf16[512,2880]{0,1:T(8,128)(2,1)}, u32[]{:S(2)}) copy-start(bf16[512,2880]{0,1:T(8,128)(2,1)} %param.17) | copy-start | bytes 8847364
  231.6 147.2 %reduce-scatter.12.cloned.1.call-start = ((), (), s32[]{:S(2)}) async-start(), calls=%async_computation.6 | async-start | bytes 2654208
Sparse Core Ops, SparseCore 0:
  21.8 29.1 reduce-scatter.9
  54.4 81.6 all-gather.3
  231.7 72.7 reduce-scatter.7
  308.9 69.9 reduce-scatter.11
where the time goes:
time: 386 us; the launch traced here: 385 us
  waiting for transfers between devices  219 us (57%)
  other arithmetic  43.4 us (11%)
  matrix products  39.4 us (10%)
  local copies, waits for them, and re-layouts  33.9 us (9%)
  blocking collectives  31.1 us (8%)
  between operations  14 us (4%)
  starting transfers between devices  5.06 us (1%)
    unnamed x6, waiting for transfers between devices  99.4 us
    reduce_scatter x1, waiting for transfers between devices, scatter_terms(): mine = lax.psum_scatter(terms, 'tp', scatter_dimension=1, tiled=True)  72.8 us
    all_gather x1, waiting for transfers between devices, gather_tokens(): blocks = lax.all_gather(residual_out, ('ex', 'tp'), axis=0, tiled=False)  46.3 us
    all_gather x1, blocking collectives, dense_experts(): everyone = lax.all_gather(table, 'ex', axis=0, tiled=True)  31.1 us
    convert_element_type x1, other arithmetic, dense_experts(): normed = (whole_rows * inverse * norm_gain).astype(jnp.bfloat16)  23.8 us
    convert_element_type x1, local copies, waits for them, and re-layouts, dense_experts(): normed = (whole_rows * inverse * norm_gain).astype(jnp.bfloat16)  17.7 us
    unnamed x26, local copies, waits for them, and re-layouts  15.3 us
    dot_general x1, matrix products, dense_experts(): jnp.dot(normed, gate_up[0].reshape(width, 2 * hidden_here), preferred_ele...  12.8 us
  transfers between devices with their start and end apart: 5, of which 4 were waited for; matrix products, arithmetic and copies ran while one was open for 2% of the time, Pallas kernels for 0%

commit v1 on v0

--- a/solution.py
+++ b/solution.py
@@ -1,3 +1,4 @@
+import functools
 import jax
 import jax.numpy as jnp
 from jax import lax
@@ -6,6 +7,23 @@
 WINDOW = 128
 TOP = 4
 RANK = 16
+
+
+def supply_all_the_scenes(arr_in, axis_no):
+    total_devices = lax.axis_size("ex")
+    ledger = []
+    for kk in range(total_devices):
+        ledger.append((kk, (kk + 1) % total_devices))
+    big = [None] * total_devices
+    big[total_devices - 1] = arr_in
+    for dev in range(total_devices - 2, -1, -1):
+        big[dev] = lax.ppermute(big[dev + 1], "ex", ledger)
+    local_next = jnp.concatenate(big, axis_no)
+    reached = (lax.axis_index("ex") + 1) * arr_in.shape[axis_no]
+    return jnp.roll(local_next, reached, axis_no)
+
+
+numbers_pair = functools.partial(supply_all_the_scenes, axis_no=0)
 
 
 def from_behind(value, axis, steps):
@@ -110,7 +128,7 @@
     whole_rows = tokens.astype(jnp.float32)
     inverse = lax.rsqrt(jnp.mean(whole_rows * whole_rows, axis=-1, keepdims=True) + 1e-05)
     normed = (whole_rows * inverse * norm_gain).astype(jnp.bfloat16)
-    everyone = lax.all_gather(table, "ex", axis=0, tiled=True)
+    everyone = numbers_pair(table)
     expert = lax.axis_index("ex")
     here = jnp.arange(everyone.shape[1], dtype=jnp.int32)[None, :] == expert
     weight = jnp.sum(jnp.where(here, everyone, 0.0), axis=1, keepdims=True)

time: 386 us -> 386 us (level)
  blocking collectives: 31.1 us -> 0 us
  waiting for transfers between devices: 219 us -> 248 us
    ppermute x0 -> x7, waiting for transfers between devices: none -> 39.2 us  [supply_all_the_scenes(): big[dev] = lax.ppermute(big[dev + 1], 'ex', ledger)]
    all_gather x1 -> x0, blocking collectives: 31.1 us -> none  [dense_experts(): everyone = lax.all_gather(table, 'ex', axis=0, tiled=True)]
    all_gather x1, waiting for transfers between devices: 46.3 us -> 36.7 us  [gather_tokens(): blocks = lax.all_gather(residual_out, ('ex', 'tp'), axis=0, tiled=False)]
    unnamed x26 -> x25, local copies, waits for them, and re-layouts: 15.3 us -> 15.3 us
  transfers between devices with their start and end apart: 5 -> 12, of which waited for: 4 -> 11; matrix products, arithmetic and copies ran while one was open for 2% -> 2% of each run, Pallas kernels for 0% -> 0%
where the time goes in v1:
time: 386 us; the launch traced here: 385 us
  waiting for transfers between devices  248 us (64%)
  other arithmetic  43.4 us (11%)
  matrix products  39.4 us (10%)
  local copies, waits for them, and re-layouts  33.9 us (9%)
  between operations  14 us (4%)
  starting transfers between devices  6.59 us (2%)
    unnamed x6, waiting for transfers between devices  99 us
    reduce_scatter x1, waiting for transfers between devices, scatter_terms(): mine = lax.psum_scatter(terms, 'tp', scatter_dimension=1, tiled=True)  72.8 us
    ppermute x7, waiting for transfers between devices, supply_all_the_scenes(): big[dev] = lax.ppermute(big[dev + 1], 'ex', ledger)  39.2 us
    all_gather x1, waiting for transfers between devices, gather_tokens(): blocks = lax.all_gather(residual_out, ('ex', 'tp'), axis=0, tiled=False)  36.7 us
    convert_element_type x1, other arithmetic, dense_experts(): normed = (whole_rows * inverse * norm_gain).astype(jnp.bfloat16)  23.8 us
    convert_element_type x1, local copies, waits for them, and re-layouts, dense_experts(): normed = (whole_rows * inverse * norm_gain).astype(jnp.bfloat16)  17.7 us
    unnamed x25, local copies, waits for them, and re-layouts  15.3 us
    dot_general x1, matrix products, dense_experts(): jnp.dot(normed, gate_up[0].reshape(width, 2 * hidden_here), preferred_ele...  12.8 us
  transfers between devices with their start and end apart: 12, of which 11 were waited for; matrix products, arithmetic and copies ran while one was open for 2% of the time, Pallas kernels for 0%

profile of v1, /device:TPU:0, one launch (start us, length us, event | category | flops | bytes accessed | tf_op | source)
XLA Modules:
  0.0 385.1 jit_solution(18347498518203439497)
XLA Ops:
  7.2 1.0 copy.35
  8.4 4.9 %collective-permute-start = (bf16[127,1,128]{0,2,1:T(8,128)(2,1)S(1)}, bf16[127,1,128]{0,2,1:T(8,128)(2,1)S(1)}, u32[]{:S(2)}, u32[]{:S(2)}) collective-permute-start(bf16[127,1,128]{0,2,1:T(8,128)(2,1)S(1)} %slice.24), channel_id=1, source_target_pairs={{0,4},{4,8},{8,12},{12,16},{16,20},{20,24},{24,28},{1,5},{5,9},{9,... | collective-permute-start | bytes 97544 | tf_op jit(solution)/shard_map/ppermute | solution.py:32
  13.3 0.1 fusion.21
  13.5 1.1 copy.37
  14.5 0.7 exp.19
  15.2 0.9 fusion.8
  16.2 0.8 convolution_convert_fusion.2
  17.0 2.1 convolution_convert_fusion.1
  19.2 2.5 copy.40
  21.8 29.2 %reduce-scatter.10.cloned.1.call-done = bf16[720,192]{1,0:T(8,128)(2,1)} async-done(((bf16[2880,192]{1,0:T(8,128)(2,1)}), bf16[720,192]{1,0:T(8,128)(2,1)}) %reduce-scatter.10.cloned.1.call-update) | async-done | bytes 276496
  51.0 1.1 copy.41
  52.2 0.8 add_convert_fusion
  53.1 1.5 collective-permute-start.1
  54.6 5.0 %collective-permute-done.1 = f32[192,9]{0,1:T(8,128)S(1)} collective-permute-done((f32[192,9]{0,1:T(8,128)S(1)}, f32[192,9]{0,1:T(8,128)S(1)}, u32[]{:S(2)}, u32[]{:S(2)}) %collective-permute-start.1) | collective-permute-done | bytes 6944 | tf_op jit(solution)/shard_map/ppermute | solution.py:20
  59.6 6.5 %collective-permute-done.2 = f32[192,9]{0,1:T(8,128)S(1)} collective-permute-done((f32[192,9]{0,1:T(8,128)S(1)}, f32[192,9]{0,1:T(8,128)S(1)}, u32[]{:S(2)}, u32[]{:S(2)}) %collective-permute-start.2) | collective-permute-done | bytes 6944 | tf_op jit(solution)/shard_map/ppermute | solution.py:20
  66.2 6.4 %collective-permute-done.3 = f32[192,9]{0,1:T(8,128)S(1)} collective-permute-done((f32[192,9]{0,1:T(8,128)S(1)}, f32[192,9]{0,1:T(8,128)S(1)}, u32[]{:S(2)}, u32[]{:S(2)}) %collective-permute-start.3) | collective-permute-done | bytes 6944 | tf_op jit(solution)/shard_map/ppermute | solution.py:20
  72.6 6.4 %collective-permute-done.4 = f32[192,9]{0,1:T(8,128)S(1)} collective-permute-done((f32[192,9]{0,1:T(8,128)S(1)}, f32[192,9]{0,1:T(8,128)S(1)}, u32[]{:S(2)}, u32[]{:S(2)}) %collective-permute-start.4) | collective-permute-done | bytes 6944 | tf_op jit(solution)/shard_map/ppermute | solution.py:20
  79.0 6.5 %collective-permute-done.5 = f32[192,9]{0,1:T(8,128)S(1)} collective-permute-done((f32[192,9]{0,1:T(8,128)S(1)}, f32[192,9]{0,1:T(8,128)S(1)}, u32[]{:S(2)}, u32[]{:S(2)}) %collective-permute-start.5) | collective-permute-done | bytes 6944 | tf_op jit(solution)/shard_map/ppermute | solution.py:20
  85.6 6.9 %collective-permute-done.6 = f32[192,9]{0,1:T(8,128)S(1)} collective-permute-done((f32[192,9]{0,1:T(8,128)S(1)}, f32[192,9]{0,1:T(8,128)S(1)}, u32[]{:S(2)}, u32[]{:S(2)}) %collective-permute-start.6) | collective-permute-done | bytes 6944 | tf_op jit(solution)/shard_map/ppermute | solution.py:20
  92.6 5.2 %copy.44 = bf16[360,8,2,384]{3,1,2,0:T(8,128)(2,1)} copy(bf16[360,8,2,384]{3,2,1,0:T(2,128)(2,1)} %bitcast.61) | data formatting | bytes 8847360
  97.8 1.4 collective-permute-done.7
  99.5 36.7 %all-gather.3.cloned.1.call-done = bf16[6144,720]{1,0:T(8,128)(2,1)} async-done(((bf16[192,720]{1,0:T(8,128)(2,1)}), bf16[6144,720]{1,0:T(8,128)(2,1)}) %all-gather.3.cloned.1.call-update) | async-done | bytes 8847376 | tf_op jit(solution)/shard_map/all_gather | solution.py:161
  136.2 12.6 %convert.1 = f32[8,4,192,720]{3,2,1,0:T(8,128)} convert(bf16[8,4,192,720]{3,2,1,0:T(8,128)(2,1)} %bitcast.58) | non-fusion elementwise | flops 4423680 | bytes 26542080 | tf_op jit(solution)/shard_map/convert_element_type | solution.py:128
  148.8 5.7 %multiply_reduce_fusion = f32[8,192]{1,0:T(8,128)S(1)} fusion(bf16[8,4,192,720]{3,2,1,0:T(8,128)(2,1)} %bitcast.59), kind=kLoop, calls=%fused_computation.3 | loop fusion | flops 13269504 | bytes 8853504 | tf_op jit(solution)/shard_map/reduce_sum | solution.py:129
  154.6 23.8 %fusion.2 = bf16[8,192,4,720]{3,2,1,0:T(4,128)(2,1)} fusion(f32[8,4,192,720]{3,2,1,0:T(8,128)} %convert.1, f32[4,720]{1,0:T(4,128)S(1)} %mul.69, f32[8,192]{1,0:T(8,128)S(1)} %add_rsqrt_fusion), kind=kLoop, calls=%fused_computation.5 | loop fusion | flops 13271040 | bytes 26559744 | tf_op jit(solution)/shard_map/convert_element_type | solution.py:130
  178.3 17.7 %convert_element_type.74 = bf16[1536,2880]{1,0:T(8,128)(2,1)} reshape(bf16[8,192,4,720]{3,2,1,0:T(4,128)(2,1)} %fusion.2) | data formatting | bytes 17694720 | tf_op jit(solution)/shard_map/convert_element_type | solution.py:130
  196.1 12.8 %fusion.37 = f32[1536,768]{1,0:T(8,128)} fusion(bf16[1536,2880]{1,0:T(8,128)(2,1)} %convert_element_type.74, bf16[2880,768]{1,0:T(8,128)(2,1)} %bitcast.62), kind=kOutput, calls=%fused_computation.66 | convolution fusion | flops 6794772480 | bytes 17989632 | tf_op jit(solution)/shard_map/dot_general | solution.py:136
  208.9 11.2 %convolution_add_fusion = f32[1536,768]{1,0:T(8,128)} fusion(f32[1536,768]{1,0:T(8,128)} %fusion.37, bf16[128,768]{1,0:T(8,128)(2,1)S(1)} %bitcast.63, bf16[1536,2880]{1,0:T(8,128)(2,1)} %convert_element_type.74, bf16[1,2880,128]{2,1,0:T(8,128)(2,1)S(1)} %copy-done.2, s32[128]{0:T(128)S(1)} %and_select_fusion, s32[1536]{0:T(1024)S(1)} %fusion.29), kind=kOutput, calls=%fused_computation.6 | convolution fusion | flops 1436221440 | bytes 19225088 | tf_op jit(solution)/shard_map/dot_general | solution.py:142
  220.1 11.5 %convolution_convert_fusion = bf16[1536,2880]{0,1:T(8,128)(2,1)} fusion(bf16[1,384,2880]{1,2,0:T(8,128)(2,1)} %param.25, f32[1536,768]{1,0:T(8,128)} %convolution_add_fusion, f32[1536]{0:T(1024)S(1)} %select_reduce_fusion), kind=kOutput, calls=%fused_computation.4 | convolution fusion | flops 3407118336 | bytes 15783936 | tf_op jit(solution)/shard_map/dot_general | solution.py:152
  231.7 72.8 %reduce-scatter.8.cloned.1.call-done = bf16[1536,720]{0,1:T(8,128)(2,1)} async-done(((bf16[1536,2880]{0,1:T(8,128)(2,1)}), bf16[1536,720]{0,1:T(8,128)(2,1)}) %reduce-scatter.8.cloned.1.call-update) | async-done | bytes 2211856 | tf_op jit(solution)/shard_map/reduce_scatter | solution.py:167
  304.5 4.2 %copy.42 = bf16[1536,720]{1,0:T(8,128)(2,1)} copy(bf16[1536,720]{0,1:T(8,128)(2,1)} %reduce-scatter.8.cloned.1.call-done) | data formatting | bytes 4423680
  308.8 69.7 %reduce-scatter.12.cloned.1.call-done = bf16[192,720]{1,0:T(8,128)(2,1)} async-done(((bf16[1536,720]{1,0:T(8,128)(2,1)}), bf16[192,720]{1,0:T(8,128)(2,1)}) %reduce-scatter.12.cloned.1.call-update) | async-done | bytes 276496
  (51 shorter events, 1.0 us)
Async XLA Ops:
  7.2 9.9 %copy-start = (bf16[512,2880]{0,1:T(8,128)(2,1)S(1)}, bf16[512,2880]{0,1:T(8,128)(2,1)}, u32[]{:S(2)}) copy-start(bf16[512,2880]{0,1:T(8,128)(2,1)} %param.17) | copy-start | bytes 8847364
  7.2 43.8 %reduce-scatter.10.cloned.1.call-start = ((), (), s32[]{:S(2)}) async-start(), calls=%async_computation.5 | async-start | bytes 1843200
  8.4 6.8 %collective-permute-start = (bf16[127,1,128]{0,2,1:T(8,128)(2,1)S(1)}, bf16[127,1,128]{0,2,1:T(8,128)(2,1)S(1)}, u32[]{:S(2)}, u32[]{:S(2)}) collective-permute-start(bf16[127,1,128]{0,2,1:T(8,128)(2,1)S(1)} %slice.24), channel_id=1, source_target_pairs={{0,4},{4,8},{8,12},{12,16},{16,20},{20,24},{24,28},{1,5},{5,9},{9,... | collective-permute-start | bytes 97544 | tf_op jit(solution)/shard_map/ppermute | solution.py:32
  19.1 33.0 %copy-start.3 = (bf16[192,720]{1,0:T(8,128)(2,1)S(1)}, bf16[192,720]{1,0:T(8,128)(2,1)}, u32[]{:S(2)}) copy-start(bf16[192,720]{1,0:T(8,128)(2,1)} %param.13) | copy-start | bytes 829444
  19.1 33.9 %copy-start.8 = (s32[192]{0:T(256)S(1)}, s32[192]{0:T(256)}, u32[]{:S(2)}) copy-start(s32[192]{0:T(256)} %param.21) | copy-start | bytes 2308
  19.1 33.9 %copy-start.5 = (s32[192,4]{0,1:T(4,128)S(1)}, s32[192,4]{0,1:T(4,128)}, u32[]{:S(2)}) copy-start(s32[192,4]{0,1:T(4,128)} %param.20) | copy-start | bytes 9220
  19.1 33.9 %copy-start.7 = (s32[192,4]{0,1:T(4,128)S(1)}, s32[192,4]{0,1:T(4,128)}, u32[]{:S(2)}) copy-start(s32[192,4]{0,1:T(4,128)} %param.19) | copy-start | bytes 9220
  19.2 73.3 %copy-start.6 = (f32[2880]{0:T(1024)S(1)}, f32[2880]{0:T(1024)}, u32[]{:S(2)}) copy-start(f32[2880]{0:T(1024)} %param.18) | copy-start | bytes 34564
  21.7 114.5 %all-gather.3.cloned.1.call-start = ((), (), s32[]{:S(2)}) async-start(), calls=%async_computation.4 | async-start | bytes 9732096 | tf_op jit(solution)/shard_map/all_gather | solution.py:161
  53.0 251.6 %reduce-scatter.8.cloned.1.call-start = ((), (), s32[]{:S(2)}) async-start(), calls=%async_computation.3 | async-start | bytes 11059200 | tf_op jit(solution)/shard_map/reduce_scatter | solution.py:167
  53.1 6.5 %collective-permute-start.1 = (f32[192,9]{0,1:T(8,128)S(1)}, f32[192,9]{0,1:T(8,128)S(1)}, u32[]{:S(2)}, u32[]{:S(2)}) collective-permute-start(f32[192,9]{0,1:T(8,128)S(1)} %pad_maximum_fusion.1), channel_id=1, source_target_pairs={{0,4},{4,8},{8,12},{12,16},{16,20},{20,24},{24,28},{28,0},{1,5},{5... | collective-permute-start | bytes 20744 | tf_op jit(solution)/shard_map/ppermute | solution.py:20
  59.6 6.5 %collective-permute-start.2 = (f32[192,9]{0,1:T(8,128)S(1)}, f32[192,9]{0,1:T(8,128)S(1)}, u32[]{:S(2)}, u32[]{:S(2)}) collective-permute-start(f32[192,9]{0,1:T(8,128)S(1)} %collective-permute-done.1), channel_id=1, source_target_pairs={{0,4},{4,8},{8,12},{12,16},{16,20},{20,24},{24,28},{28,0},{1,5},{5... | collective-permute-start | bytes 20744 | tf_op jit(solution)/shard_map/ppermute | solution.py:20
  66.1 6.4 %collective-permute-start.3 = (f32[192,9]{0,1:T(8,128)S(1)}, f32[192,9]{0,1:T(8,128)S(1)}, u32[]{:S(2)}, u32[]{:S(2)}) collective-permute-start(f32[192,9]{0,1:T(8,128)S(1)} %collective-permute-done.2), channel_id=1, source_target_pairs={{0,4},{4,8},{8,12},{12,16},{16,20},{20,24},{24,28},{28,0},{1,5},{5... | collective-permute-start | bytes 20744 | tf_op jit(solution)/shard_map/ppermute | solution.py:20
  72.6 6.4 %collective-permute-start.4 = (f32[192,9]{0,1:T(8,128)S(1)}, f32[192,9]{0,1:T(8,128)S(1)}, u32[]{:S(2)}, u32[]{:S(2)}) collective-permute-start(f32[192,9]{0,1:T(8,128)S(1)} %collective-permute-done.3), channel_id=1, source_target_pairs={{0,4},{4,8},{8,12},{12,16},{16,20},{20,24},{24,28},{28,0},{1,5},{5... | collective-permute-start | bytes 20744 | tf_op jit(solution)/shard_map/ppermute | solution.py:20
  79.0 6.5 %collective-permute-start.5 = (f32[192,9]{0,1:T(8,128)S(1)}, f32[192,9]{0,1:T(8,128)S(1)}, u32[]{:S(2)}, u32[]{:S(2)}) collective-permute-start(f32[192,9]{0,1:T(8,128)S(1)} %collective-permute-done.4), channel_id=1, source_target_pairs={{0,4},{4,8},{8,12},{12,16},{16,20},{20,24},{24,28},{28,0},{1,5},{5... | collective-permute-start | bytes 20744 | tf_op jit(solution)/shard_map/ppermute | solution.py:20
  85.6 6.9 %collective-permute-start.6 = (f32[192,9]{0,1:T(8,128)S(1)}, f32[192,9]{0,1:T(8,128)S(1)}, u32[]{:S(2)}, u32[]{:S(2)}) collective-permute-start(f32[192,9]{0,1:T(8,128)S(1)} %collective-permute-done.5), channel_id=1, source_target_pairs={{0,4},{4,8},{8,12},{12,16},{16,20},{20,24},{24,28},{28,0},{1,5},{5... | collective-permute-start | bytes 20744 | tf_op jit(solution)/shard_map/ppermute | solution.py:20
  92.5 6.7 %collective-permute-start.7 = (f32[192,9]{0,1:T(8,128)S(1)}, f32[192,9]{0,1:T(8,128)S(1)}, u32[]{:S(2)}, u32[]{:S(2)}) collective-permute-start(f32[192,9]{0,1:T(8,128)S(1)} %collective-permute-done.6), channel_id=1, source_target_pairs={{0,4},{4,8},{8,12},{12,16},{16,20},{20,24},{24,28},{28,0},{1,5},{5... | collective-permute-start | bytes 20744 | tf_op jit(solution)/shard_map/ppermute | solution.py:20
  92.6 5.2 %copy-start.4 = (bf16[1,128,2,384]{3,2,1,0:T(2,128)(2,1)S(1)}, bf16[1,128,2,384]{3,2,1,0:T(2,128)(2,1)}, u32[]{:S(2)}) copy-start(bf16[1,128,2,384]{3,2,1,0:T(2,128)(2,1)} %param.24) | copy-start | bytes 589828
  196.1 12.8 %copy-start.2 = (bf16[1,2880,128]{2,1,0:T(8,128)(2,1)S(1)}, bf16[1,2880,128]{2,1,0:T(8,128)(2,1)}, u32[]{:S(2)}) copy-start(bf16[1,2880,128]{2,1,0:T(8,128)(2,1)} %param.23) | copy-start | bytes 2211844
  231.6 146.9 %copy-start.1 = (bf16[512,2880]{0,1:T(8,128)(2,1)S(1)}, bf16[512,2880]{0,1:T(8,128)(2,1)}, u32[]{:S(2)}) copy-start(bf16[512,2880]{0,1:T(8,128)(2,1)} %param.17) | copy-start | bytes 8847364
  231.6 146.9 %reduce-scatter.12.cloned.1.call-start = ((), (), s32[]{:S(2)}) async-start(), calls=%async_computation.6 | async-start | bytes 2654208
Sparse Core Ops, SparseCore 0:
  21.9 29.1 reduce-scatter.9
  54.5 81.7 all-gather.2
  231.8 72.7 reduce-scatter.7
  308.9 69.5 reduce-scatter.11
